TPU v7x, 256 devices: a whole 4x4x8 slice. The times are simulated.
256 devices in a mesh: rec: 32 (over z, y), src: 8 (over x, core).
Axes of the slice: x: 4, y: 4, z: 8, core: 2. Of those that a mesh axis runs over, the one named last changes fastest.
Arguments:
- kernel: float32 [2, 2, 5120, 5120], P(None, None, 'rec', 'src'), may hold values from -0.0625 to 0.0625
- traces: float32 [8, 896, 2, 2, 256], P('src', 'rec')
- acq_lists: int32 [8, 896], P('src', 'rec'), may hold values from 0 to 639, as said below
- counts: int32 [8, 32], P('src', 'rec'), may hold values from 1 to 28, as said below
Outputs:
- solution: float32 [5120, 2, 2, 256], P(('src', 'rec'))
- next_left: float32 [5120, 2, 2, 256], P(('rec', 'src'))
Inputs may be any that keep to these rules, and one draw needn't show every extreme that they name: `acq_lists`: an id a * 20 + k names row k of area a. Within each list the first counts[s, r] slots of the blocks name every id exactly once; other slots hold ids to be ignored. No block names more than 1 ids of one area, and every block that names an area names exactly 1 of its ids. `counts`: used slots of a block; in every list some block uses all 28.
All inputs are finite; a program needn't handle non-finite values.
Results may differ from a plain program's by a relative error of at most 0.00026.
Values sent between devices are 32-bit elements; how exact they have to be, the bound alone decides.
A program may use at most 64 MiB of HBM per device.

v0:
```python
import jax
import jax.numpy as jnp
from jax import lax
from jax.sharding import PartitionSpec as P

NR = 5120
FREQS = 2
SOURCES = 256
ITERS = 2


def kernel_apply(kernel, vector):
    highest = lax.Precision.HIGHEST
    real_part = jnp.einsum("fmc,cfn->mfn", kernel[0], vector[:, 0], precision=highest) - jnp.einsum(
        "fmc,cfn->mfn", kernel[1], vector[:, 1], precision=highest
    )
    imag_part = jnp.einsum("fmc,cfn->mfn", kernel[0], vector[:, 1], precision=highest) + jnp.einsum(
        "fmc,cfn->mfn", kernel[1], vector[:, 0], precision=highest
    )
    return jnp.stack([real_part, imag_part], axis=1)


def kernel_adjoint(kernel, vector):
    highest = lax.Precision.HIGHEST
    real_part = jnp.einsum("fmc,mfn->cfn", kernel[0], vector[:, 0], precision=highest) + jnp.einsum(
        "fmc,mfn->cfn", kernel[1], vector[:, 1], precision=highest
    )
    imag_part = jnp.einsum("fmc,mfn->cfn", kernel[0], vector[:, 1], precision=highest) - jnp.einsum(
        "fmc,mfn->cfn", kernel[1], vector[:, 0], precision=highest
    )
    return jnp.stack([real_part, imag_part], axis=1)


def widen(values):
    return values[None, None, :, None]


def rms_norm(vector):
    local_sum = jnp.sum(vector * vector, axis=(0, 1, 3))
    global_sum = lax.psum(local_sum, ("rec", "src"))
    return jnp.sqrt(global_sum / (2.0 * NR * SOURCES))


def on_device(kernel, traces, acq_lists, counts):
    highest = lax.Precision.HIGHEST
    my_area = lax.axis_index("rec")
    row_count = kernel.shape[2] // lax.axis_size("src")
    slot_count = traces.shape[1]
    width = traces.shape[2] * traces.shape[3] * traces.shape[4]
    row_iota = jnp.arange(row_count, dtype=jnp.int32)
    piece_traces = lax.all_gather(traces, "rec", axis=1, tiled=True)
    piece_ids = lax.all_gather(acq_lists, "rec", axis=1, tiled=True)
    piece_counts = lax.all_gather(counts, "rec", axis=1, tiled=True)
    span_slots = piece_ids.shape[1]
    slot_iota = jnp.arange(span_slots, dtype=jnp.int32)
    block_iota = jnp.arange(piece_counts.shape[1], dtype=jnp.int32)
    in_block = (slot_iota // slot_count)[:, None] == block_iota[None, :]
    limits = jnp.sum(jnp.where(in_block, piece_counts[0][None, :], 0), axis=1)
    filled = slot_iota % slot_count < limits
    list_ids = piece_ids[0]
    wanted = filled & (list_ids // row_count == my_area)
    selector = ((list_ids % row_count)[None, :] == row_iota[:, None]) & wanted[None, :]
    observed = jnp.dot(
        selector.astype(jnp.float32), piece_traces.reshape(span_slots, width), precision=highest
    )
    observed = observed.reshape(row_count, 2, FREQS, SOURCES)

    def adjoint(vector):
        spread = lax.all_gather(vector, "src", axis=0, tiled=True)
        return lax.psum_scatter(
            kernel_adjoint(kernel, spread), "rec", scatter_dimension=0, tiled=True
        )

    beta_norm = rms_norm(observed)
    left_unit = observed / widen(beta_norm)
    right_vec = adjoint(left_unit)
    alpha_norm = rms_norm(right_vec)
    right_unit = right_vec / widen(alpha_norm)
    search = right_unit
    solution = jnp.zeros(right_unit.shape, jnp.float32)
    phibar = beta_norm
    rhobar = alpha_norm
    next_left = observed
    for iteration in range(ITERS):
        forward_spread = lax.all_gather(right_unit, "rec", axis=0, tiled=True)
        next_left = (
            lax.psum_scatter(
                kernel_apply(kernel, forward_spread), "src", scatter_dimension=0, tiled=True
            )
            - widen(alpha_norm) * left_unit
        )
        beta_norm = rms_norm(next_left)
        left_unit = next_left / widen(beta_norm)
        rho_value = jnp.sqrt(rhobar * rhobar + beta_norm * beta_norm)
        cosine = rhobar / rho_value
        sine_value = beta_norm / rho_value
        phi_value = cosine * phibar
        phibar = sine_value * phibar
        solution = solution + widen(phi_value / rho_value) * search
        if iteration + 1 < ITERS:
            right_vec = adjoint(left_unit) - widen(beta_norm) * right_unit
            alpha_norm = rms_norm(right_vec)
            right_unit = right_vec / widen(alpha_norm)
            theta_value = sine_value * alpha_norm
            rhobar = -cosine * alpha_norm
            search = right_unit - widen(theta_value / rho_value) * search
    return (solution, next_left)


def solution(mesh):
    placed = (
        P(None, None, "rec", "src"),
        P("src", "rec", None, None, None),
        P("src", "rec"),
        P("src", "rec"),
    )
    return jax.shard_map(
        on_device,
        mesh=mesh,
        in_specs=placed,
        out_specs=(P(("src", "rec"), None, None, None), P(("rec", "src"), None, None, None)),
        check_vma=False,
    )
```

profile of v0, /device:TPU:1, one launch (start us, length us, event | category | flops | bytes accessed | tf_op | source)
XLA Modules:
  0.0 1147.3 jit_solution(5020311262918664336)
XLA Ops:
  12.1 20.3 %all-reduce.6 = (s32[896]{0:T(1024)S(1)}, s32[32]{0:T(128)S(1)}) all-reduce(s32[896]{0:T(1024)S(1)} %bitcast_dynamic-update-slice_fusion.1, s32[32]{0:T(128)S(1)} %bitcast_dynamic-update-slice_fusion), channel_id=1, replica_groups=mesh['rec'=32,'src'=8] {'rec'}, use_global_device_ids=true, to_apply=%add | all-reduce | flops 928 | bytes 7424
  32.6 59.6 %all-gather.4.cloned.1.call-done = f32[1,896,2,2,256]{4,3,2,0,1:T(2,128)} async-done(((f32[1,28,2,2,256]{4,3,2,0,1:T(2,128)}), f32[1,896,2,2,256]{4,3,2,0,1:T(2,128)}) %all-gather.4.cloned.1.call-update) | async-done | bytes 3670032 | tf_op jit(solution)/shard_map/all_gather | solution.py:51
  92.1 6.6 copy.66
  98.8 3.9 multiply_reduce_fusion.3
  102.7 77.6 %psum.35 = f32[2]{0:T(128)S(1)} all-reduce(f32[2]{0:T(128)S(1)} %get-tuple-element.32), channel_id=1, replica_groups=mesh['rec'=32,'src'=8] {'rec','src'}, use_global_device_ids=true, to_apply=%region_2.3 | all-reduce | flops 2 | bytes 16 | tf_op jit(solution)/shard_map/psum | solution.py:40
  180.4 14.0 %all_gather.24 = f32[160,2,2,256]{3,2,1,0:T(2,128)S(1)} all-gather(f32[20,2,2,256]{3,2,1,0:T(2,128)S(1)} %copy.43), channel_id=1, replica_groups=mesh['rec'=32,'src'=8] {'src'}, dimensions={0}, use_global_device_ids=true | all-gather | bytes 737280 | tf_op jit(solution)/shard_map/all_gather | solution.py:69
  200.6 1.7 pad_maximum_fusion
  202.3 5.1 copy.46
  208.2 146.3 %all-reduce.12.cloned.1.call-done = f32[640,2,2,256]{3,2,1,0:T(2,128)} async-done(((f32[640,2,2,256]{3,2,1,0:T(2,128)}), f32[640,2,2,256]{3,2,1,0:T(2,128)}) %all-reduce.12.cloned.1.call-update) | async-done | bytes 2621456
  355.6 78.4 %psum.36 = f32[2]{0:T(128)S(1)} all-reduce(f32[2]{0:T(128)S(1)} %get-tuple-element.17), channel_id=1, replica_groups=mesh['rec'=32,'src'=8] {'rec','src'}, use_global_device_ids=true, to_apply=%region_5.6 | all-reduce | flops 2 | bytes 16 | tf_op jit(solution)/shard_map/psum | solution.py:40
  435.0 71.0 %all-gather.6.cloned.1.call-done = f32[640,2,2,256]{3,2,1,0:T(2,128)} async-done(((f32[20,2,2,256]{3,2,1,0:T(2,128)}), f32[640,2,2,256]{3,2,1,0:T(2,128)}) %all-gather.6.cloned.1.call-update) | async-done | bytes 2621456 | tf_op jit(solution)/shard_map/all_gather | solution.py:85
  506.0 2.6 fusion.73
  516.0 63.6 %all-reduce.14.cloned.1.call-done = f32[160,2,2,256]{3,2,1,0:T(2,128)} async-done(((f32[160,2,2,256]{3,2,1,0:T(2,128)}), f32[160,2,2,256]{3,2,1,0:T(2,128)}) %all-reduce.14.cloned.1.call-update) | async-done | bytes 655376
  580.7 78.5 %psum.37 = f32[2]{0:T(128)S(1)} all-reduce(f32[2]{0:T(128)S(1)} %multiply_reduce_fusion.2), channel_id=1, replica_groups=mesh['rec'=32,'src'=8] {'rec','src'}, use_global_device_ids=true, to_apply=%region_8.9 | all-reduce | flops 2 | bytes 16 | tf_op jit(solution)/shard_map/psum | solution.py:40
  659.4 14.2 %all_gather.26 = f32[160,2,2,256]{3,2,1,0:T(2,128)S(1)} all-gather(f32[20,2,2,256]{3,2,1,0:T(2,128)S(1)} %copy.53), channel_id=1, replica_groups=mesh['rec'=32,'src'=8] {'src'}, dimensions={0}, use_global_device_ids=true | all-gather | bytes 737280 | tf_op jit(solution)/shard_map/all_gather | solution.py:69
  678.2 1.5 fusion.3
  679.7 1.7 pad_maximum_fusion.1
  681.4 5.1 copy.56
  686.6 147.7 %all-reduce.16.cloned.1.call-done = f32[640,2,2,256]{3,2,1,0:T(2,128)} async-done(((f32[640,2,2,256]{3,2,1,0:T(2,128)}), f32[640,2,2,256]{3,2,1,0:T(2,128)}) %all-reduce.16.cloned.1.call-update) | async-done | bytes 2621456
  835.4 78.4 %psum.38 = f32[2]{0:T(128)S(1)} all-reduce(f32[2]{0:T(128)S(1)} %multiply_reduce_fusion.1), channel_id=1, replica_groups=mesh['rec'=32,'src'=8] {'rec','src'}, use_global_device_ids=true, to_apply=%region_11.12 | all-reduce | flops 2 | bytes 16 | tf_op jit(solution)/shard_map/psum | solution.py:40
  914.9 70.9 %all-gather.8.cloned.1.call-done = f32[640,2,2,256]{3,2,1,0:T(2,128)} async-done(((f32[20,2,2,256]{3,2,1,0:T(2,128)}), f32[640,2,2,256]{3,2,1,0:T(2,128)}) %all-gather.8.cloned.1.call-update) | async-done | bytes 2621456 | tf_op jit(solution)/shard_map/all_gather | solution.py:85
  985.8 2.6 fusion.72
  994.5 64.9 %all-reduce.18.cloned.1.call-done = f32[160,2,2,256]{3,2,1,0:T(2,128)} async-done(((f32[160,2,2,256]{3,2,1,0:T(2,128)}), f32[160,2,2,256]{3,2,1,0:T(2,128)}) %all-reduce.18.cloned.1.call-update) | async-done | bytes 655376
  1060.5 78.5 %psum.39 = f32[2]{0:T(128)S(1)} all-reduce(f32[2]{0:T(128)S(1)} %get-tuple-element.15), channel_id=1, replica_groups=mesh['rec'=32,'src'=8] {'rec','src'}, use_global_device_ids=true, to_apply=%region_14.15 | all-reduce | flops 2 | bytes 16 | tf_op jit(solution)/shard_map/psum | solution.py:40
  (75 shorter events, 35.4 us)
Async XLA Ops:
  7.2 85.0 %all-gather.4.cloned.1.call-start = ((), (), s32[]{:S(2)}) async-start(), calls=%async_computation | async-start | bytes 3784704 | tf_op jit(solution)/shard_map/all_gather | solution.py:51
  7.9 346.6 %all-reduce.12.cloned.1.call-start = ((), (), s32[]{:S(2)}) async-start(), calls=%async_computation.3 | async-start | bytes 5242880
  102.7 92.0 %copy-start = (f32[2,2,160,640]{3,2,1,0:T(8,128)S(1)}, f32[2,2,160,640]{3,2,1,0:T(8,128)}, u32[]{:S(2)}) copy-start(f32[2,2,160,640]{3,2,1,0:T(8,128)} %param.4) | copy-start | bytes 4915204
  207.5 298.6 %all-gather.6.cloned.1.call-start = ((), (), s32[]{:S(2)}) async-start(), calls=%async_computation.1 | async-start | bytes 2703360 | tf_op jit(solution)/shard_map/all_gather | solution.py:85
  434.8 144.9 %all-reduce.14.cloned.1.call-start = ((), (), s32[]{:S(2)}) async-start(), calls=%async_computation.4 | async-start | bytes 1310720
  513.3 1.5 copy-start.1
  514.7 319.6 %all-reduce.16.cloned.1.call-start = ((), (), s32[]{:S(2)}) async-start(), calls=%async_computation.5 | async-start | bytes 5242880
  686.6 299.3 %all-gather.8.cloned.1.call-start = ((), (), s32[]{:S(2)}) async-start(), calls=%async_computation.2 | async-start | bytes 2703360 | tf_op jit(solution)/shard_map/all_gather | solution.py:85
  914.6 144.8 %all-reduce.18.cloned.1.call-start = ((), (), s32[]{:S(2)}) async-start(), calls=%async_computation.6 | async-start | bytes 1310720
Sparse Core Ops, SparseCore 0:
  10.6 81.5 all-gather.3
  207.6 146.8 all-reduce.11
  434.9 71.0 all-gather.5
  514.8 64.7 all-reduce.13
  686.7 147.5 all-reduce.15
  914.7 71.0 all-gather.7
  994.6 64.7 all-reduce.17
where the time goes:
time: 1150 us
  waiting for transfers between devices  625 us (54%)
  blocking collectives  440 us (38%)
  local copies, waits for them, and re-layouts  34.2 us (3%)
  matrix products  24.8 us (2%)
  between operations  17 us (1%)
    unnamed x11, waiting for transfers between devices  423 us
    psum x5, blocking collectives, rms_norm(): global_sum = lax.psum(local_sum, ('rec', 'src'))  391 us
    all_gather x2, waiting for transfers between devices, on_device(): forward_spread = lax.all_gather(right_unit, 'rec', axis=0, tiled=True)  142 us
    all_gather x1, waiting for transfers between devices, on_device(): piece_traces = lax.all_gather(traces, 'rec', axis=1, tiled=True)  59.6 us
    all_gather x2, blocking collectives, adjoint(): spread = lax.all_gather(vector, 'src', axis=0, tiled=True)  28.2 us
  transfers between devices with their start and end apart: 7, of which 7 were waited for; matrix products, arithmetic and copies ran while one was open for 0% of the time, Pallas kernels for 0%

commit v1 on v0

--- a/solution.py
+++ b/solution.py
@@ -82,7 +82,11 @@
     rhobar = alpha_norm
     next_left = observed
     for iteration in range(ITERS):
-        forward_spread = lax.all_gather(right_unit, "rec", axis=0, tiled=True)
+        devices = lax.axis_size("rec")
+        repeats = [devices if d == 0 else 1 for d in range(right_unit.ndim)]
+        forward_spread = lax.all_to_all(
+            jnp.tile(right_unit, repeats), "rec", split_axis=0, concat_axis=0, tiled=True
+        )
         next_left = (
             lax.psum_scatter(
                 kernel_apply(kernel, forward_spread), "src", scatter_dimension=0, tiled=True

time: 1150 us -> 1140 us (level)
  waiting for transfers between devices: 625 us -> 474 us
  blocking collectives: 440 us -> 574 us
    all_gather x2 -> x0, waiting for transfers between devices: 142 us -> none  [on_device(): forward_spread = lax.all_gather(right_unit, 'rec', axis=0, tiled=True)]
    all_to_all x0 -> x2, blocking collectives: none -> 133 us  [on_device(): lax.all_to_all(jnp.tile(right_unit, repeats), 'rec', split_axis=0, concat...]
    unnamed x11 -> x9, waiting for transfers between devices: 423 us -> 414 us
  transfers between devices with their start and end apart: 7 -> 5, of which waited for: 7 -> 5; matrix products, arithmetic and copies ran while one was open for 0% -> 0% of each run, Pallas kernels for 0% -> 0%
where the time goes in v1:
time: 1140 us; the launch traced here: 1130 us
  blocking collectives  574 us (50%)
  waiting for transfers between devices  474 us (42%)
  local copies, waits for them, and re-layouts  31.8 us (3%)
  matrix products  24.8 us (2%)
  between operations  16.9 us (1%)
    unnamed x9, waiting for transfers between devices  414 us
    psum x5, blocking collectives, rms_norm(): global_sum = lax.psum(local_sum, ('rec', 'src'))  392 us
    all_to_all x2, blocking collectives, on_device(): lax.all_to_all(jnp.tile(right_unit, repeats), 'rec', split_axis=0, concat...  133 us
    all_gather x1, waiting for transfers between devices, on_device(): piece_traces = lax.all_gather(traces, 'rec', axis=1, tiled=True)  59.6 us
    all_gather x2, blocking collectives, adjoint(): spread = lax.all_gather(vector, 'src', axis=0, tiled=True)  28.2 us
  transfers between devices with their start and end apart: 5, of which 5 were waited for; matrix products, arithmetic and copies ran while one was open for 0% of the time, Pallas kernels for 0%

profile of v1, /device:TPU:1, one launch (start us, length us, event | category | flops | bytes accessed | tf_op | source)
XLA Modules:
  0.0 1127.3 jit_solution(918189334637589336)
XLA Ops:
  12.1 20.3 %all-reduce.6 = (s32[896]{0:T(1024)S(1)}, s32[32]{0:T(128)S(1)}) all-reduce(s32[896]{0:T(1024)S(1)} %bitcast_dynamic-update-slice_fusion.1, s32[32]{0:T(128)S(1)} %bitcast_dynamic-update-slice_fusion), channel_id=1, replica_groups=mesh['rec'=32,'src'=8] {'rec'}, use_global_device_ids=true, to_apply=%add | all-reduce | flops 928 | bytes 7424
  32.6 59.6 %all-gather.2.cloned.1.call-done = f32[1,896,2,2,256]{4,3,2,0,1:T(2,128)} async-done(((f32[1,28,2,2,256]{4,3,2,0,1:T(2,128)}), f32[1,896,2,2,256]{4,3,2,0,1:T(2,128)}) %all-gather.2.cloned.1.call-update) | async-done | bytes 3670032 | tf_op jit(solution)/shard_map/all_gather | solution.py:51
  92.1 6.6 copy.81
  98.8 3.9 multiply_reduce_fusion.3
  102.7 77.6 %psum.35 = f32[2]{0:T(128)S(1)} all-reduce(f32[2]{0:T(128)S(1)} %get-tuple-element.34), channel_id=1, replica_groups=mesh['rec'=32,'src'=8] {'rec','src'}, use_global_device_ids=true, to_apply=%region_2.3 | all-reduce | flops 2 | bytes 16 | tf_op jit(solution)/shard_map/psum | solution.py:40
  180.4 14.0 %all_gather.18 = f32[160,2,2,256]{3,2,1,0:T(2,128)S(1)} all-gather(f32[20,2,2,256]{3,2,1,0:T(2,128)S(1)} %copy.58), channel_id=1, replica_groups=mesh['rec'=32,'src'=8] {'src'}, dimensions={0}, use_global_device_ids=true | all-gather | bytes 737280 | tf_op jit(solution)/shard_map/all_gather | solution.py:69
  197.6 1.5 fusion.4
  199.1 1.5 fusion.5
  200.6 1.7 pad_maximum_fusion
  202.3 5.1 copy.61
  208.2 146.3 %all-reduce.12.cloned.1.call-done = f32[640,2,2,256]{3,2,1,0:T(2,128)} async-done(((f32[640,2,2,256]{3,2,1,0:T(2,128)}), f32[640,2,2,256]{3,2,1,0:T(2,128)}) %all-reduce.12.cloned.1.call-update) | async-done | bytes 2621456
  355.6 78.9 %psum.36 = f32[2]{0:T(128)S(1)} all-reduce(f32[2]{0:T(128)S(1)} %get-tuple-element.19), channel_id=1, replica_groups=mesh['rec'=32,'src'=8] {'rec','src'}, use_global_device_ids=true, to_apply=%region_5.6 | all-reduce | flops 2 | bytes 16 | tf_op jit(solution)/shard_map/psum | solution.py:40
  435.8 66.6 %all_to_all.10 = f32[640,2,2,256]{3,2,1,0:T(2,128)S(1)} all-to-all(f32[640,2,2,256]{3,2,1,0:T(2,128)S(1)} %bitcast.141), channel_id=1, replica_groups=mesh['rec'=32,'src'=8] {'rec'}, dimensions={0} | all-to-all | bytes 5242880 | tf_op jit(solution)/shard_map/all_to_all | solution.py:87
  510.7 59.1 %all-reduce.14.cloned.1.call-done = f32[160,2,2,256]{3,2,1,0:T(2,128)} async-done(((f32[160,2,2,256]{3,2,1,0:T(2,128)}), f32[160,2,2,256]{3,2,1,0:T(2,128)}) %all-reduce.14.cloned.1.call-update) | async-done | bytes 655376
  570.9 78.5 %psum.37 = f32[2]{0:T(128)S(1)} all-reduce(f32[2]{0:T(128)S(1)} %multiply_reduce_fusion.2), channel_id=1, replica_groups=mesh['rec'=32,'src'=8] {'rec','src'}, use_global_device_ids=true, to_apply=%region_8.9 | all-reduce | flops 2 | bytes 16 | tf_op jit(solution)/shard_map/psum | solution.py:40
  649.5 14.2 %all_gather.19 = f32[160,2,2,256]{3,2,1,0:T(2,128)S(1)} all-gather(f32[20,2,2,256]{3,2,1,0:T(2,128)S(1)} %copy.68), channel_id=1, replica_groups=mesh['rec'=32,'src'=8] {'src'}, dimensions={0}, use_global_device_ids=true | all-gather | bytes 737280 | tf_op jit(solution)/shard_map/all_gather | solution.py:69
  666.8 1.5 fusion.2
  669.8 1.7 pad_maximum_fusion.1
  671.5 5.1 copy.71
  676.7 147.8 %all-reduce.16.cloned.1.call-done = f32[640,2,2,256]{3,2,1,0:T(2,128)} async-done(((f32[640,2,2,256]{3,2,1,0:T(2,128)}), f32[640,2,2,256]{3,2,1,0:T(2,128)}) %all-reduce.16.cloned.1.call-update) | async-done | bytes 2621456
  825.6 78.4 %psum.38 = f32[2]{0:T(128)S(1)} all-reduce(f32[2]{0:T(128)S(1)} %multiply_reduce_fusion.1), channel_id=1, replica_groups=mesh['rec'=32,'src'=8] {'rec','src'}, use_global_device_ids=true, to_apply=%region_11.12 | all-reduce | flops 2 | bytes 16 | tf_op jit(solution)/shard_map/psum | solution.py:40
  905.3 66.8 %all_to_all.11 = f32[640,2,2,256]{3,2,1,0:T(2,128)S(1)} all-to-all(f32[640,2,2,256]{3,2,1,0:T(2,128)S(1)} %bitcast.142), channel_id=1, replica_groups=mesh['rec'=32,'src'=8] {'rec'}, dimensions={0} | all-to-all | bytes 5242880 | tf_op jit(solution)/shard_map/all_to_all | solution.py:87
  979.0 60.4 %all-reduce.18.cloned.1.call-done = f32[160,2,2,256]{3,2,1,0:T(2,128)} async-done(((f32[160,2,2,256]{3,2,1,0:T(2,128)}), f32[160,2,2,256]{3,2,1,0:T(2,128)}) %all-reduce.18.cloned.1.call-update) | async-done | bytes 655376
  1040.6 78.5 %psum.39 = f32[2]{0:T(128)S(1)} all-reduce(f32[2]{0:T(128)S(1)} %get-tuple-element.17), channel_id=1, replica_groups=mesh['rec'=32,'src'=8] {'rec','src'}, use_global_device_ids=true, to_apply=%region_14.15 | all-reduce | flops 2 | bytes 16 | tf_op jit(solution)/shard_map/psum | solution.py:40
  (73 shorter events, 34.8 us)
Async XLA Ops:
  7.2 85.0 %all-gather.2.cloned.1.call-start = ((), (), s32[]{:S(2)}) async-start(), calls=%async_computation.2 | async-start | bytes 3784704 | tf_op jit(solution)/shard_map/all_gather | solution.py:51
  7.9 346.6 %all-reduce.12.cloned.1.call-start = ((), (), s32[]{:S(2)}) async-start(), calls=%async_computation.3 | async-start | bytes 5242880
  102.7 92.0 %copy-start = (f32[2,2,160,640]{3,2,1,0:T(8,128)S(1)}, f32[2,2,160,640]{3,2,1,0:T(8,128)}, u32[]{:S(2)}) copy-start(f32[2,2,160,640]{3,2,1,0:T(8,128)} %param.4) | copy-start | bytes 4915204
  207.5 362.3 %all-reduce.14.cloned.1.call-start = ((), (), s32[]{:S(2)}) async-start(), calls=%async_computation.4 | async-start | bytes 1310720
  508.0 1.5 copy-start.1
  509.4 315.1 %all-reduce.16.cloned.1.call-start = ((), (), s32[]{:S(2)}) async-start(), calls=%async_computation.5 | async-start | bytes 5242880
  676.7 362.8 %all-reduce.18.cloned.1.call-start = ((), (), s32[]{:S(2)}) async-start(), calls=%async_computation.6 | async-start | bytes 1310720
Sparse Core Ops, SparseCore 0:
  10.6 81.5 all-gather.1
  207.6 146.8 all-reduce.11
  509.5 60.2 all-reduce.13
  676.8 147.6 all-reduce.15
  979.2 60.2 all-reduce.17
